TPU v7x, 32 devices: a whole 2x2x4 slice. The times are simulated.
32 devices in a mesh: dp: 8 (over y, x, core), mp: 4 (over z).
Axes of the slice: x: 2, y: 2, z: 4, core: 2. Of those that a mesh axis runs over, the one named last changes fastest.
Arguments:
- tokens: bfloat16 [16384, 1024], P(('dp', 'mp')), may hold values from -6 to 6
- segments: int32 [16384], P('dp'), may hold values from 0 to 68, as said below
- ln1_gain: bfloat16 [1024], replicated, may hold values from 0.5 to 1.5
- ln1_bias: bfloat16 [1024], replicated, may hold values from -1.75 to 1.75
- w_query: bfloat16 [1024, 1024], P(None, 'mp'), may hold values from -0.1875 to 0.1875
- b_query: bfloat16 [1024], P('mp'), may hold values from -3 to 3
- w_key: bfloat16 [1024, 1024], P(None, 'mp'), may hold values from -0.1875 to 0.1875
- w_value: bfloat16 [1024, 1024], P(None, 'mp'), may hold values from -0.1875 to 0.1875
- b_value: bfloat16 [1024], P('mp'), may hold values from -3 to 3
- w_out: bfloat16 [1024, 1024], P('mp'), may hold values from -0.5 to 0.5
- b_out: bfloat16 [1024], replicated, may hold values from -1.75 to 1.75
- ln2_gain: bfloat16 [1024], replicated, may hold values from 0.5 to 1.5
- ln2_bias: bfloat16 [1024], replicated, may hold values from -1.75 to 1.75
- w_up: bfloat16 [1024, 4096], P(None, 'mp'), may hold values from -0.1875 to 0.1875
- b_up: bfloat16 [4096], P('mp'), may hold values from -3 to 3
- w_down: bfloat16 [4096, 1024], P('mp'), may hold values from -0.09375 to 0.09375
- b_down: bfloat16 [1024], replicated, may hold values from -1.75 to 1.75
- cotangent: bfloat16 [16384, 1024], P(('dp', 'mp')), may hold values from -6 to 6
Outputs:
- output: bfloat16 [16384, 1024], P(('dp', 'mp'))
- grad_tokens: float32 [16384, 1024], P(('dp', 'mp'))
- grad_ln1_gain: float32 [1024], replicated
- grad_ln1_bias: float32 [1024], replicated
- grad_w_query: float32 [1024, 1024], P(None, 'mp')
- grad_b_query: float32 [1024], P('mp')
- grad_w_key: float32 [1024, 1024], P(None, 'mp')
- grad_w_value: float32 [1024, 1024], P(None, 'mp')
- grad_b_value: float32 [1024], P('mp')
- grad_w_out: float32 [1024, 1024], P('mp')
- grad_b_out: float32 [1024], replicated
- grad_ln2_gain: float32 [1024], replicated
- grad_ln2_bias: float32 [1024], replicated
- grad_w_up: float32 [1024, 4096], P(None, 'mp')
- grad_b_up: float32 [4096], P('mp')
- grad_w_down: float32 [4096, 1024], P('mp')
- grad_b_down: float32 [1024], replicated
Inputs may be any that keep to these rules, and one draw needn't show every extreme that they name: `segments`: within each group of 2048 rows the ids start at 0 and rise by one from image to image, so an image's patches are consecutive rows. Small images have 30 to 48 patches; in some groups, and always in at least one, the first image has exactly 900 patches; in at least one other group every image has exactly 30 patches; the last image of a group may have fewer patches. No image has more than 900 patches.
All inputs are finite; a program needn't handle non-finite values.
Results may differ from a plain program's by a relative error of at most 0.019.
Values may be sent and summed in bfloat16 or wider, within the bound.
A program may use at most 128 MiB of HBM per device.

v0:
```python
import jax
import jax.numpy as jnp
from jax import lax
from jax.sharding import PartitionSpec as P

HEAD_DIM = 64
epsilon = 1e-06
minus_big = -1e30


def matmul(left, right):
    return jnp.dot(left, right, preferred_element_type=jnp.float32)


def times_transposed(left, right):
    return lax.dot_general(
        left, right, (((1,), (1,)), ((), ())), preferred_element_type=jnp.float32
    )


def transposed_times(left, right):
    return lax.dot_general(
        left, right, (((0,), (0,)), ((), ())), preferred_element_type=jnp.float32
    )


def normalize(values):
    average = jnp.mean(values, axis=1, keepdims=True)
    centered = values - average
    spread = jnp.mean(centered * centered, axis=1, keepdims=True)
    inv_std = lax.rsqrt(spread + epsilon)
    return (centered * inv_std, inv_std)


def norm_back(grad_norm, x_hat, inv_std, gain_vec):
    grad_hat = grad_norm * gain_vec
    first = jnp.mean(grad_hat, axis=1, keepdims=True)
    second = jnp.mean(grad_hat * x_hat, axis=1, keepdims=True)
    grad_input = inv_std * (grad_hat - first - x_hat * second)
    return (grad_input, jnp.sum(grad_norm * x_hat, axis=0), jnp.sum(grad_norm, axis=0))


def gelu_slope(values):
    cdf_part = 0.5 * (1.0 + lax.erf(values * 0.7071067811865476))
    return cdf_part + values * jnp.exp(-0.5 * values * values) * 0.3989422804014327


def local(
    tokens,
    segments,
    ln1_gain,
    ln1_bias,
    w_query,
    b_query,
    w_key,
    w_value,
    b_value,
    w_out,
    b_out,
    ln2_gain,
    ln2_bias,
    w_up,
    b_up,
    w_down,
    b_down,
    cotangent,
):
    all_rows = segments.shape[0]
    local_width = w_query.shape[1]
    head_count = local_width // HEAD_DIM
    score_scale = HEAD_DIM ** (-0.5)
    block_rows = min(512, all_rows)
    block_count = all_rows // block_rows
    gain_one = ln1_gain.astype(jnp.float32)
    bias_one = ln1_bias.astype(jnp.float32)
    gain_two = ln2_gain.astype(jnp.float32)
    bias_two = ln2_bias.astype(jnp.float32)
    resid_in = tokens.astype(jnp.float32)
    hat_one, inv_one = normalize(resid_in)
    normed_one = (hat_one * gain_one + bias_one).astype(jnp.bfloat16)
    gathered_one = lax.all_gather(normed_one, "mp", axis=0, tiled=True)
    query = (matmul(gathered_one, w_query) + b_query.astype(jnp.float32)).astype(jnp.bfloat16)
    keys = matmul(gathered_one, w_key).astype(jnp.bfloat16)
    values = (matmul(gathered_one, w_value) + b_value.astype(jnp.float32)).astype(jnp.bfloat16)
    query_blocks = query.reshape(block_count, block_rows, head_count, HEAD_DIM)
    segment_blocks = segments.reshape(block_count, block_rows)
    keys_heads = keys.reshape(all_rows, head_count, HEAD_DIM)
    values_heads = values.reshape(all_rows, head_count, HEAD_DIM)

    def scores_of(query_block, segment_block):
        raw_scores = (
            jnp.einsum("qhd,khd->hqk", query_block, keys_heads, preferred_element_type=jnp.float32)
            * score_scale
        )
        same_image = (segment_block[:, None] == segments[None, :])[None]
        return jnp.where(same_image, raw_scores, minus_big)

    def forward_block(pieces):
        query_block, segment_block = pieces
        scores = scores_of(query_block, segment_block)
        row_max = jnp.max(scores, axis=2, keepdims=True)
        exp_scores = jnp.exp(scores - row_max)
        row_sum = jnp.sum(exp_scores, axis=2, keepdims=True)
        probabilities = (exp_scores / row_sum).astype(jnp.bfloat16)
        head_out = jnp.einsum(
            "hqk,khd->qhd", probabilities, values_heads, preferred_element_type=jnp.float32
        )
        return (head_out.astype(jnp.bfloat16), row_max[:, :, 0] + jnp.log(row_sum[:, :, 0]))

    attn_blocks, log_totals = lax.map(forward_block, (query_blocks, segment_blocks))
    attn_out = attn_blocks.reshape(all_rows, local_width)
    attn_branch = lax.psum_scatter(
        matmul(attn_out, w_out).astype(jnp.bfloat16), "mp", scatter_dimension=0, tiled=True
    ).astype(jnp.float32)
    hidden_one = resid_in + attn_branch + b_out.astype(jnp.float32)
    hat_two, inv_two = normalize(hidden_one)
    normed_two = (hat_two * gain_two + bias_two).astype(jnp.bfloat16)
    gathered_two = lax.all_gather(normed_two, "mp", axis=0, tiled=True)
    upper = matmul(gathered_two, w_up) + b_up.astype(jnp.float32)
    active = jax.nn.gelu(upper, approximate=False).astype(jnp.bfloat16)
    mlp_branch = lax.psum_scatter(
        matmul(active, w_down).astype(jnp.bfloat16), "mp", scatter_dimension=0, tiled=True
    ).astype(jnp.float32)
    output = (hidden_one + mlp_branch + b_down.astype(jnp.float32)).astype(jnp.bfloat16)
    grad_out = cotangent.astype(jnp.float32)
    grad_b_down = jnp.sum(grad_out, axis=0)
    grad_rows = lax.all_gather(cotangent, "mp", axis=0, tiled=True)
    grad_w_down = transposed_times(active, grad_rows)
    grad_active = times_transposed(grad_rows, w_down)
    grad_upper = (grad_active * gelu_slope(upper)).astype(jnp.bfloat16)
    grad_b_up = jnp.sum(grad_upper, axis=0, dtype=jnp.float32)
    grad_w_up = transposed_times(gathered_two, grad_upper)
    grad_normed_two = lax.psum_scatter(
        times_transposed(grad_upper, w_up).astype(jnp.bfloat16),
        "mp",
        scatter_dimension=0,
        tiled=True,
    ).astype(jnp.float32)
    grad_hidden, grad_ln2_gain, grad_ln2_bias = norm_back(
        grad_normed_two, hat_two, inv_two, gain_two
    )
    grad_hidden = grad_hidden + grad_out
    grad_b_out = jnp.sum(grad_hidden, axis=0)
    hidden_rows = lax.all_gather(grad_hidden.astype(jnp.bfloat16), "mp", axis=0, tiled=True)
    grad_w_out = transposed_times(attn_out, hidden_rows)
    grad_attn = times_transposed(hidden_rows, w_out).astype(jnp.bfloat16)
    grad_attn_blocks = grad_attn.reshape(block_count, block_rows, head_count, HEAD_DIM)

    def backward_block(carry, pieces):
        grad_keys_sum, grad_values_sum = carry
        query_block, segment_block, log_block, grad_block = pieces
        scores = scores_of(query_block, segment_block)
        probabilities = jnp.exp(scores - log_block[:, :, None])
        grad_probs = jnp.einsum(
            "qhd,khd->hqk", grad_block, values_heads, preferred_element_type=jnp.float32
        )
        inner = jnp.sum(probabilities * grad_probs, axis=2, keepdims=True)
        grad_scores = (probabilities * (grad_probs - inner)).astype(jnp.bfloat16)
        grad_query_block = (
            jnp.einsum("hqk,khd->qhd", grad_scores, keys_heads, preferred_element_type=jnp.float32)
            * score_scale
        )
        grad_keys_sum = (
            grad_keys_sum
            + jnp.einsum(
                "hqk,qhd->khd", grad_scores, query_block, preferred_element_type=jnp.float32
            )
            * score_scale
        )
        grad_values_sum = grad_values_sum + jnp.einsum(
            "hqk,qhd->khd",
            probabilities.astype(jnp.bfloat16),
            grad_block,
            preferred_element_type=jnp.float32,
        )
        return ((grad_keys_sum, grad_values_sum), grad_query_block.astype(jnp.bfloat16))

    zeros_heads = jnp.zeros((all_rows, head_count, HEAD_DIM), jnp.float32)
    (grad_keys_sum, grad_values_sum), grad_query_blocks = lax.scan(
        backward_block,
        (zeros_heads, zeros_heads),
        (query_blocks, segment_blocks, log_totals, grad_attn_blocks),
    )
    grad_query = grad_query_blocks.reshape(all_rows, local_width)
    grad_keys = grad_keys_sum.reshape(all_rows, local_width).astype(jnp.bfloat16)
    grad_values = grad_values_sum.reshape(all_rows, local_width).astype(jnp.bfloat16)
    grad_w_query = transposed_times(gathered_one, grad_query)
    grad_b_query = jnp.sum(grad_query, axis=0, dtype=jnp.float32)
    grad_w_key = transposed_times(gathered_one, grad_keys)
    grad_w_value = transposed_times(gathered_one, grad_values)
    grad_b_value = jnp.sum(grad_values, axis=0, dtype=jnp.float32)
    term = times_transposed(grad_query, w_query)
    term = term + times_transposed(grad_keys, w_key)
    grad_normed_one = lax.psum_scatter(
        (term + times_transposed(grad_values, w_value)).astype(jnp.bfloat16),
        "mp",
        scatter_dimension=0,
        tiled=True,
    ).astype(jnp.float32)
    grad_input, grad_ln1_gain, grad_ln1_bias = norm_back(
        grad_normed_one, hat_one, inv_one, gain_one
    )
    grad_tokens = grad_input + grad_hidden
    (
        grad_w_query,
        grad_b_query,
        grad_w_key,
        grad_w_value,
        grad_b_value,
        grad_w_out,
        grad_w_up,
        grad_b_up,
        grad_w_down,
    ) = (
        lax.psum(grad_w_query.astype(jnp.bfloat16), "dp").astype(jnp.float32),
        lax.psum(grad_b_query.astype(jnp.bfloat16), "dp").astype(jnp.float32),
        lax.psum(grad_w_key.astype(jnp.bfloat16), "dp").astype(jnp.float32),
        lax.psum(grad_w_value.astype(jnp.bfloat16), "dp").astype(jnp.float32),
        lax.psum(grad_b_value.astype(jnp.bfloat16), "dp").astype(jnp.float32),
        lax.psum(grad_w_out.astype(jnp.bfloat16), "dp").astype(jnp.float32),
        lax.psum(grad_w_up.astype(jnp.bfloat16), "dp").astype(jnp.float32),
        lax.psum(grad_b_up.astype(jnp.bfloat16), "dp").astype(jnp.float32),
        lax.psum(grad_w_down.astype(jnp.bfloat16), "dp").astype(jnp.float32),
    )
    grad_ln1_gain, grad_ln1_bias, grad_b_out, grad_ln2_gain, grad_ln2_bias, grad_b_down = lax.psum(
        (grad_ln1_gain, grad_ln1_bias, grad_b_out, grad_ln2_gain, grad_ln2_bias, grad_b_down),
        ("dp", "mp"),
    )
    return (
        output,
        grad_tokens,
        grad_ln1_gain,
        grad_ln1_bias,
        grad_w_query,
        grad_b_query,
        grad_w_key,
        grad_w_value,
        grad_b_value,
        grad_w_out,
        grad_b_out,
        grad_ln2_gain,
        grad_ln2_bias,
        grad_w_up,
        grad_b_up,
        grad_w_down,
        grad_b_down,
    )


def solution(mesh):
    in_specs = (
        P(("dp", "mp"), None),
        P("dp"),
        P(),
        P(),
        P(None, "mp"),
        P("mp"),
        P(None, "mp"),
        P(None, "mp"),
        P("mp"),
        P("mp", None),
        P(),
        P(),
        P(),
        P(None, "mp"),
        P("mp"),
        P("mp", None),
        P(),
        P(("dp", "mp"), None),
    )
    out_specs = (
        P(("dp", "mp"), None),
        P(("dp", "mp"), None),
        P(),
        P(),
        P(None, "mp"),
        P("mp"),
        P(None, "mp"),
        P(None, "mp"),
        P("mp"),
        P("mp", None),
        P(),
        P(),
        P(),
        P(None, "mp"),
        P("mp"),
        P("mp", None),
        P(),
    )
    return jax.shard_map(local, mesh=mesh, in_specs=in_specs, out_specs=out_specs, check_vma=False)
```

profile of v0, /device:TPU:0, one launch (start us, length us, event | category | flops | bytes accessed | tf_op | source)
XLA Modules:
  0.0 1142.3 jit_solution(16438787603620042261)
XLA Ops:
  14.7 83.5 %all-gather.5.cloned.1.call-done = bf16[2048,1024]{1,0:T(8,128)(2,1)} async-done(((bf16[512,1024]{1,0:T(8,128)(2,1)}), bf16[2048,1024]{1,0:T(8,128)(2,1)}) %all-gather.5.cloned.1.call-update) | async-done | bytes 4194320 | tf_op jit(solution)/shard_map/all_gather | solution.py:81
  114.7 64.4 %while.27 = (s32[]{:T(128)}, bf16[4,512,4,64]{1,3,2,0:T(8,128)(2,1)}, f32[4,4,512]{2,1,0:T(4,128)}, s32[4,512]{1,0:T(4,128)S(1)}, s32[2048]{0:T(1024)S(1)}, /*in...) while((s32[]{:T(128)}, ...), condition=%wide.region_5.6_spmd, body=%wide.region_2.5_spmd.sunk | while | flops 1125251072 | bytes 57227380 | solution.py:110
  186.8 74.8 %reduce-scatter.5.cloned.1.call-done = bf16[512,1024]{1,0:T(8,128)(2,1)} async-done(((bf16[2048,1024]{1,0:T(8,128)(2,1)}), bf16[512,1024]{1,0:T(8,128)(2,1)}) %reduce-scatter.5.cloned.1.call-update) | async-done | bytes 1048592 | tf_op jit(solution)/shard_map/reduce_scatter | solution.py:112
  267.4 80.8 %all-gather.7.cloned.1.call-done = bf16[2048,1024]{1,0:T(8,128)(2,1)} async-done(((bf16[512,1024]{1,0:T(8,128)(2,1)}), bf16[2048,1024]{1,0:T(8,128)(2,1)}) %all-gather.7.cloned.1.call-update) | async-done | bytes 4194320 | tf_op jit(solution)/shard_map/all_gather | solution.py:118
  348.2 25.0 %fusion.45 = (bf16[2048,1024]{1,0:T(8,128)(2,1)}, f32[2048,1024]{1,0:T(8,128)}) fusion(f32[1024]{0:T(1024)S(1)} %convert_element_type.187, bf16[2048,1024]{1,0:T(8,128)(2,1)} %all-gather.7.cloned.1.call-done, bf16[1024,1024]{1,0:T(8,128)(2,1)S(1)} %copy-done), kind=kOutput, calls=%fused_computation.56 | convolution fusion | flops 4433379328 | bytes 18878464 | tf_op jit(solution)/shard_map/dot_general | solution.py:12
  373.2 55.6 %all-gather.9.cloned.1.call-done = bf16[2048,1024]{1,0:T(8,128)(2,1)} async-done(((bf16[512,1024]{1,0:T(8,128)(2,1)}), bf16[2048,1024]{1,0:T(8,128)(2,1)}) %all-gather.9.cloned.1.call-update) | async-done | bytes 4194320 | tf_op jit(solution)/shard_map/all_gather | solution.py:127
  428.9 11.9 %fusion.87 = (bf16[1024]{0:T(1024)(128)(2,1)}, bf16[2048,1024]{1,0:T(8,128)(2,1)S(1)}) fusion(f32[2048,1024]{1,0:T(8,128)} %get-tuple-element.270, f32[1024]{0:T(1024)S(1)} %convert_element_type.187, bf16[2048,1024]{1,0:T(8,128)(2,1)} %all-gather.9.cloned.1.call-done, bf16[1024,1024]{1,0:T(8,128)(2,1)} %param.37), kind=kOutput, calls=%fused_computation.143 | convolution fusion | flops 4320132096 | bytes 18880512 | tf_op jit(solution)/shard_map/dot_general | solution.py:16
  450.5 8.3 convolution_convert_fusion.2
  459.5 64.9 %reduce-scatter.9.cloned.1.call-done = bf16[512,1024]{1,0:T(8,128)(2,1)} async-done(((bf16[2048,1024]{1,0:T(8,128)(2,1)}), bf16[512,1024]{1,0:T(8,128)(2,1)}) %reduce-scatter.9.cloned.1.call-update) | async-done | bytes 1048592 | tf_op jit(solution)/shard_map/reduce_scatter | solution.py:133
  527.4 76.5 %reduce-scatter.7.cloned.1.call-done = bf16[512,1024]{1,0:T(8,128)(2,1)} async-done(((bf16[2048,1024]{1,0:T(8,128)(2,1)}), bf16[512,1024]{1,0:T(8,128)(2,1)}) %reduce-scatter.7.cloned.1.call-update) | async-done | bytes 1048592 | tf_op jit(solution)/shard_map/reduce_scatter | solution.py:121
  610.6 9.5 convolution_convert_fusion.5
  625.9 66.0 %all-gather.11.cloned.1.call-done = bf16[2048,1024]{1,0:T(8,128)(2,1)} async-done(((bf16[512,1024]{1,0:T(8,128)(2,1)}), bf16[2048,1024]{1,0:T(8,128)(2,1)}) %all-gather.11.cloned.1.call-update) | async-done | bytes 4194320 | tf_op jit(solution)/shard_map/all_gather | solution.py:144
  699.7 191.3 %while.28 = (s32[]{:T(128)}, f32[2048,4,64]{0,2,1:T(8,128)}, f32[2048,4,64]{0,2,1:T(8,128)}, bf16[4,512,4,64]{1,3,2,0:T(8,128)(2,1)}, bf16[4,512,4,64]{1,3,2,0:T...) while((s32[]{:T(128)}, f32[2048,4,64]{0,2,1:T(8,128)}, ...), condition=%wide.region_15.16_spmd.clone, body=%wide.region_13.15_spmd.clone.sunk | while | flops 2751199232 | bytes 176625968 | solution.py:179
  706.3 7.3 fusion.167
  713.5 11.3 multiply_reduce_fusion.3
  724.8 10.8 multiply_convert_fusion.2
  735.7 7.1 fusion.168
  753.1 7.7 fusion.167
  760.7 11.3 multiply_reduce_fusion.3
  772.0 10.8 multiply_convert_fusion.2
  782.9 7.1 fusion.168
  801.0 7.7 fusion.167
  808.7 11.3 multiply_reduce_fusion.3
  820.0 10.8 multiply_convert_fusion.2
  830.8 7.1 fusion.168
  849.0 7.7 fusion.167
  856.6 11.3 multiply_reduce_fusion.3
  867.9 10.8 multiply_convert_fusion.2
  914.5 14.5 %all-reduce.1 = (bf16[256]{0:T(256)(128)(2,1)S(1)}, bf16[256]{0:T(256)(128)(2,1)S(1)}, bf16[1024]{0:T(1024)(128)(2,1)S(1)}) all-reduce(bf16[256]{0:T(256)(128)(2,1)S(1)} %reduce_sum.195, bf16[256]{0:T(256)(128)(2,1)S(1)} %reduce_sum.197, bf16[1024]{0:T(1024)(128)(2,1)S(1)} %copy-done.41), channel_id=1, replica_groups=mesh['dp'=8,'mp'=4] {'dp'}, use_global_device_ids=true, to_apply=%region_25.26 | all-reduce | flops 1536 | bytes 6144 | tf_op jit(solution)/shard_map/psum | solution.py:216
  930.7 78.0 %all-reduce.5.cloned.1.call-done = (bf16[1024,256]{1,0:T(8,128)(2,1)}, bf16[1024,256]{1,0:T(8,128)(2,1)}, bf16[1024,256]{1,0:T(8,128)(2,1)}, bf16[256,1024]{1,0:...) async-done(((bf16[1024,256]{1,0:T(8,128)(2,1)}, bf16[1024,256]{1,0:T(8,128)(2,1)}, bf16[1024,256]{1,0:T(8,128)(2,1)}, bf16[256,1024]{1,0:T(8,128)(2,1)}, ...) | async-done | bytes 6291472 | tf_op jit(solution)/shard_map/psum | solution.py:215
  1021.3 66.7 %reduce-scatter.11.cloned.1.call-done = bf16[512,1024]{1,0:T(8,128)(2,1)} async-done(((bf16[2048,1024]{1,0:T(8,128)(2,1)}), bf16[512,1024]{1,0:T(8,128)(2,1)}) %reduce-scatter.11.cloned.1.call-update) | async-done | bytes 1048592 | tf_op jit(solution)/shard_map/reduce_scatter | solution.py:194
  1090.3 41.4 %all-reduce = (f32[1024]{0:T(1024)}, f32[1024]{0:T(1024)}, f32[1024]{0:T(1024)}, f32[1024]{0:T(1024)}, f32[1024]{0:T(1024)}, /*index=5*/f32[1024]{0:T(1024)}) all-reduce(f32[1024]{0:T(1024)S(1)} %get-tuple-element.200, f32[1024]{0:T(1024)S(1)} %get-tuple-element.205, ...), channel_id=1, replica_groups=mesh['dp'=8,'mp'=4] {'dp','mp'}, use_global_device_ids=true, to_apply=%region_20.21 | all-reduce | flops 6144 | bytes 49152 | tf_op jit(solution)/shard_map/psum | solution.py:225
  (264 shorter events, 229.3 us)
Async XLA Ops:
  7.2 341.0 %copy-start = (bf16[1024,1024]{1,0:T(8,128)(2,1)S(1)}, bf16[1024,1024]{1,0:T(8,128)(2,1)}, u32[]{:S(2)}) copy-start(bf16[1024,1024]{1,0:T(8,128)(2,1)} %param.35) | copy-start | bytes 6291460
  7.2 7.4 copy-start.47
  7.2 7.4 copy-start.48
  7.2 7.4 copy-start.15
  7.2 91.0 %all-gather.5.cloned.1.call-start = ((), (), s32[]{:S(2)}) async-start(), calls=%async_computation.4 | async-start | bytes 5242880 | tf_op jit(solution)/shard_map/all_gather | solution.py:81
  14.6 247.0 %reduce-scatter.5.cloned.1.call-start = ((), (), s32[]{:S(2)}) async-start(), calls=%async_computation.5 | async-start | bytes 5242880 | tf_op jit(solution)/shard_map/reduce_scatter | solution.py:112
  186.1 75.5 %copy-start.3 = (bf16[512,1024]{1,0:T(8,128)(2,1)S(1)}, bf16[512,1024]{1,0:T(8,128)(2,1)}, u32[]{:S(2)}) copy-start(bf16[512,1024]{1,0:T(8,128)(2,1)} %param.22) | copy-start | bytes 3145732
  186.2 162.0 %all-gather.7.cloned.1.call-start = ((), (), s32[]{:S(2)}) async-start(), calls=%async_computation.6 | async-start | bytes 5242880 | tf_op jit(solution)/shard_map/all_gather | solution.py:118
  266.8 162.1 %all-gather.9.cloned.1.call-start = ((), (), s32[]{:S(2)}) async-start(), calls=%async_computation.8 | async-start | bytes 5242880 | tf_op jit(solution)/shard_map/all_gather | solution.py:127
  267.4 257.0 %reduce-scatter.9.cloned.1.call-start = ((), (), s32[]{:S(2)}) async-start(), calls=%async_computation.9 | async-start | bytes 5242880 | tf_op jit(solution)/shard_map/reduce_scatter | solution.py:133
  449.0 154.9 %reduce-scatter.7.cloned.1.call-start = ((), (), s32[]{:S(2)}) async-start(), calls=%async_computation.7 | async-start | bytes 5242880 | tf_op jit(solution)/shard_map/reduce_scatter | solution.py:121
  458.9 65.5 %copy-start.7 = (bf16[512,1024]{1,0:T(8,128)(2,1)S(1)}, bf16[512,1024]{1,0:T(8,128)(2,1)}, u32[]{:S(2)}) copy-start(bf16[512,1024]{1,0:T(8,128)(2,1)} %reduce-scatter.5.cloned.1.call-done) | copy-start | bytes 3145732
  458.9 145.0 %copy-start.12 = (bf16[512,1024]{1,0:T(8,128)(2,1)S(1)}, bf16[512,1024]{1,0:T(8,128)(2,1)}, u32[]{:S(2)}) copy-start(bf16[512,1024]{1,0:T(8,128)(2,1)} %param.39) | copy-start | bytes 3145732
  458.9 233.1 %all-gather.11.cloned.1.call-start = ((), (), s32[]{:S(2)}) async-start(), calls=%async_computation.10 | async-start | bytes 5242880 | tf_op jit(solution)/shard_map/all_gather | solution.py:144
  610.6 398.2 %all-reduce.5.cloned.1.call-start = ((), (), s32[]{:S(2)}) async-start(), calls=%async_computation.12 | async-start | bytes 12582912 | tf_op jit(solution)/shard_map/psum | solution.py:215
  610.6 9.5 copy-start.45
  610.6 9.5 copy-start.50
  620.2 71.8 %copy-start.19 = (bf16[256,1024]{1,0:T(8,128)(2,1)S(1)}, bf16[256,1024]{1,0:T(8,128)(2,1)}, u32[]{:S(2)}) copy-start(bf16[256,1024]{1,0:T(8,128)(2,1)} %param.31) | copy-start | bytes 1572868
  782.9 7.1 copy-start.2
  830.8 7.1 copy-start.2
  878.8 7.1 copy-start.2
  905.6 182.4 %reduce-scatter.11.cloned.1.call-start = ((), (), s32[]{:S(2)}) async-start(), calls=%async_computation.11 | async-start | bytes 5242880 | tf_op jit(solution)/shard_map/reduce_scatter | solution.py:194
  1008.7 7.5 copy-start.14
  1018.7 69.3 %copy-start.4 = (bf16[512,1024]{1,0:T(8,128)(2,1)S(1)}, bf16[512,1024]{1,0:T(8,128)(2,1)}, u32[]{:S(2)}) copy-start(bf16[512,1024]{1,0:T(8,128)(2,1)} %param.22) | copy-start | bytes 3145732
  1018.7 69.3 %copy-start.27 = (f32[1024]{0:T(1024)S(1)}, f32[1024]{0:T(1024)}, u32[]{:S(2)}) copy-start(f32[1024]{0:T(1024)} %copy-done.26) | copy-start | bytes 12292
  1018.7 69.3 %copy-start.29 = (f32[512]{0:T(512)S(1)}, f32[512]{0:T(512)}, u32[]{:S(2)}) copy-start(f32[512]{0:T(512)} %copy-done.28) | copy-start | bytes 6148
  1018.7 69.3 %copy-start.31 = (f32[512]{0:T(512)S(1)}, f32[512]{0:T(512)}, u32[]{:S(2)}) copy-start(f32[512]{0:T(512)} %copy-done.30) | copy-start | bytes 6148
  1018.7 71.5 %copy-start.32 = (f32[1024]{0:T(1024)S(1)}, f32[1024]{0:T(1024)}, u32[]{:S(2)}) copy-start(f32[1024]{0:T(1024)} %get-tuple-element.198) | copy-start | bytes 12292
  1018.7 71.5 %copy-start.33 = (f32[1024]{0:T(1024)S(1)}, f32[1024]{0:T(1024)}, u32[]{:S(2)}) copy-start(f32[1024]{0:T(1024)} %get-tuple-element.204) | copy-start | bytes 12292
  1018.8 71.5 %copy-start.34 = (f32[1024]{0:T(1024)S(1)}, f32[1024]{0:T(1024)}, u32[]{:S(2)}) copy-start(f32[1024]{0:T(1024)} %get-tuple-element.261) | copy-start | bytes 12292
  1018.8 71.5 %copy-start.35 = (f32[1024]{0:T(1024)S(1)}, f32[1024]{0:T(1024)}, u32[]{:S(2)}) copy-start(f32[1024]{0:T(1024)} %get-tuple-element.268) | copy-start | bytes 12292
  1018.8 116.8 %copy-start.1 = (bf16[1024,1024]{1,0:T(8,128)(2,1)S(1)}, bf16[1024,1024]{1,0:T(8,128)(2,1)}, u32[]{:S(2)}) copy-start(bf16[1024,1024]{1,0:T(8,128)(2,1)} %param.35) | copy-start | bytes 6291460
  (43 other events, 120.8 us)
Sparse Core Ops, SparseCore 0:
  14.7 83.4 all-gather.4
  186.3 75.2 reduce-scatter.4
  266.9 81.2 all-gather.6
  349.6 79.2 all-gather.8
  449.1 75.2 reduce-scatter.8
  526.5 77.2 reduce-scatter.6
  610.7 81.2 all-gather.10
  905.7 102.9 all-reduce.4
  1011.0 76.9 reduce-scatter.10
where the time goes:
time: 1150 us; the launch traced here: 1140 us
  waiting for transfers between devices  647 us (56%)
  matrix products  277 us (24%)
  other arithmetic  116 us (10%)
  blocking collectives  55.9 us (5%)
  local copies, waits for them, and re-layouts  29.5 us (3%)
  between operations  14.6 us (1%)
    all_gather x1, waiting for transfers between devices, local(): gathered_one = lax.all_gather(normed_one, 'mp', axis=0, tiled=True)  83.5 us
    all_gather x1, waiting for transfers between devices, local(): gathered_two = lax.all_gather(normed_two, 'mp', axis=0, tiled=True)  80.8 us
    psum x1, waiting for transfers between devices, local(): lax.psum(grad_w_query.astype(jnp.bfloat16), 'dp').astype(jnp.float32)  78 us
    reduce_scatter x1, waiting for transfers between devices, local(): lax.psum_scatter(matmul(active, w_down).astype(jnp.bfloat16), 'mp', scatt...  76.5 us
    reduce_scatter x1, waiting for transfers between devices, local(): lax.psum_scatter(matmul(attn_out, w_out).astype(jnp.bfloat16), 'mp', scat...  74.8 us
    reduce_scatter x1, waiting for transfers between devices, local(): lax.psum_scatter((term + times_transposed(grad_values, w_value)).astype(j...  66.7 us
    all_gather x1, waiting for transfers between devices, local(): lax.all_gather(grad_hidden.astype(jnp.bfloat16), 'mp', axis=0, tiled=True)  66 us
    reduce_scatter x1, waiting for transfers between devices, local(): lax.psum_scatter(times_transposed(grad_upper, w_up).astype(jnp.bfloat16),...  64.9 us
  transfers between devices with their start and end apart: 9, of which 9 were waited for; matrix products, arithmetic and copies ran while one was open for 6% of the time, Pallas kernels for 0%

commit v1 on v0

--- a/solution.py
+++ b/solution.py
@@ -141,7 +141,15 @@
     )
     grad_hidden = grad_hidden + grad_out
     grad_b_out = jnp.sum(grad_hidden, axis=0)
-    hidden_rows = lax.all_gather(grad_hidden.astype(jnp.bfloat16), "mp", axis=0, tiled=True)
+    value = grad_hidden.astype(jnp.bfloat16)
+    ways, here = (lax.axis_size("mp"), lax.axis_index("mp"))
+    hidden_rows, reach = (value, 1)
+    while reach < ways:
+        theirs = lax.ppermute(hidden_rows, "mp", [(d, d ^ reach) for d in range(ways)])
+        mine_first = jnp.concatenate([hidden_rows, theirs], axis=0)
+        theirs_first = jnp.concatenate([theirs, hidden_rows], axis=0)
+        hidden_rows = jnp.where(here & reach == 0, mine_first, theirs_first)
+        reach = 2 * reach
     grad_w_out = transposed_times(attn_out, hidden_rows)
     grad_attn = times_transposed(hidden_rows, w_out).astype(jnp.bfloat16)
     grad_attn_blocks = grad_attn.reshape(block_count, block_rows, head_count, HEAD_DIM)

time: 1150 us -> 1190 us (1.035)
  waiting for transfers between devices: 647 us -> 681 us
    ppermute x0 -> x2, waiting for transfers between devices: none -> 98.9 us  [local(): lax.ppermute(hidden_rows, 'mp', [(d, d ^ reach) for d in range(ways)])]
    all_gather x1 -> x0, waiting for transfers between devices: 66 us -> none  [local(): lax.all_gather(grad_hidden.astype(jnp.bfloat16), 'mp', axis=0, tiled=True)]
  transfers between devices with their start and end apart: 9 -> 10, of which waited for: 9 -> 10; matrix products, arithmetic and copies ran while one was open for 6% -> 6% of each run, Pallas kernels for 0% -> 0%
where the time goes in v1:
time: 1190 us; the launch traced here: 1180 us
  waiting for transfers between devices  681 us (57%)
  matrix products  277 us (23%)
  other arithmetic  116 us (10%)
  blocking collectives  56 us (5%)
  local copies, waits for them, and re-layouts  30.8 us (3%)
  between operations  15.1 us (1%)
    ppermute x2, waiting for transfers between devices, local(): lax.ppermute(hidden_rows, 'mp', [(d, d ^ reach) for d in range(ways)])  98.9 us
    all_gather x1, waiting for transfers between devices, local(): gathered_one = lax.all_gather(normed_one, 'mp', axis=0, tiled=True)  83.5 us
    all_gather x1, waiting for transfers between devices, local(): gathered_two = lax.all_gather(normed_two, 'mp', axis=0, tiled=True)  80.7 us
    psum x1, waiting for transfers between devices, local(): lax.psum(grad_w_query.astype(jnp.bfloat16), 'dp').astype(jnp.float32)  79.2 us
    reduce_scatter x1, waiting for transfers between devices, local(): lax.psum_scatter(matmul(active, w_down).astype(jnp.bfloat16), 'mp', scatt...  76.5 us
    reduce_scatter x1, waiting for transfers between devices, local(): lax.psum_scatter(matmul(attn_out, w_out).astype(jnp.bfloat16), 'mp', scat...  74.8 us
    reduce_scatter x1, waiting for transfers between devices, local(): lax.psum_scatter((term + times_transposed(grad_values, w_value)).astype(j...  66.7 us
    reduce_scatter x1, waiting for transfers between devices, local(): lax.psum_scatter(times_transposed(grad_upper, w_up).astype(jnp.bfloat16),...  64.9 us
  transfers between devices with their start and end apart: 10, of which 10 were waited for; matrix products, arithmetic and copies ran while one was open for 6% of the time, Pallas kernels for 0%

profile of v1, /device:TPU:0, one launch (start us, length us, event | category | flops | bytes accessed | tf_op | source)
XLA Modules:
  0.0 1182.8 jit_solution(8734353460055208783)
XLA Ops:
  14.7 83.5 %all-gather.4.cloned.1.call-done = bf16[2048,1024]{1,0:T(8,128)(2,1)} async-done(((bf16[512,1024]{1,0:T(8,128)(2,1)}), bf16[2048,1024]{1,0:T(8,128)(2,1)}) %all-gather.4.cloned.1.call-update) | async-done | bytes 4194320 | tf_op jit(solution)/shard_map/all_gather | solution.py:81
  114.7 64.4 %while.27 = (s32[]{:T(128)}, bf16[4,512,4,64]{1,3,2,0:T(8,128)(2,1)}, f32[4,4,512]{2,1,0:T(4,128)}, s32[4,512]{1,0:T(4,128)S(1)}, s32[2048]{0:T(1024)S(1)}, /*in...) while((s32[]{:T(128)}, ...), condition=%wide.region_5.6_spmd, body=%wide.region_2.5_spmd.sunk | while | flops 1125251072 | bytes 57227380 | solution.py:110
  186.9 74.8 %reduce-scatter.5.cloned.1.call-done = bf16[512,1024]{1,0:T(8,128)(2,1)} async-done(((bf16[2048,1024]{1,0:T(8,128)(2,1)}), bf16[512,1024]{1,0:T(8,128)(2,1)}) %reduce-scatter.5.cloned.1.call-update) | async-done | bytes 1048592 | tf_op jit(solution)/shard_map/reduce_scatter | solution.py:112
  267.4 80.7 %all-gather.6.cloned.1.call-done = bf16[2048,1024]{1,0:T(8,128)(2,1)} async-done(((bf16[512,1024]{1,0:T(8,128)(2,1)}), bf16[2048,1024]{1,0:T(8,128)(2,1)}) %all-gather.6.cloned.1.call-update) | async-done | bytes 4194320 | tf_op jit(solution)/shard_map/all_gather | solution.py:118
  348.2 25.0 %fusion.45 = (bf16[2048,1024]{1,0:T(8,128)(2,1)}, f32[2048,1024]{1,0:T(8,128)}) fusion(f32[1024]{0:T(1024)S(1)} %convert_element_type.187, bf16[2048,1024]{1,0:T(8,128)(2,1)} %all-gather.6.cloned.1.call-done, bf16[1024,1024]{1,0:T(8,128)(2,1)S(1)} %copy-done), kind=kOutput, calls=%fused_computation.56 | convolution fusion | flops 4433379328 | bytes 18878464 | tf_op jit(solution)/shard_map/dot_general | solution.py:12
  373.2 55.6 %all-gather.8.cloned.1.call-done = bf16[2048,1024]{1,0:T(8,128)(2,1)} async-done(((bf16[512,1024]{1,0:T(8,128)(2,1)}), bf16[2048,1024]{1,0:T(8,128)(2,1)}) %all-gather.8.cloned.1.call-update) | async-done | bytes 4194320 | tf_op jit(solution)/shard_map/all_gather | solution.py:127
  428.8 11.9 %fusion.89 = (bf16[1024]{0:T(1024)(128)(2,1)}, bf16[2048,1024]{1,0:T(8,128)(2,1)S(1)}) fusion(f32[2048,1024]{1,0:T(8,128)} %get-tuple-element.270, f32[1024]{0:T(1024)S(1)} %convert_element_type.187, bf16[2048,1024]{1,0:T(8,128)(2,1)} %all-gather.8.cloned.1.call-done, bf16[1024,1024]{1,0:T(8,128)(2,1)} %param.37), kind=kOutput, calls=%fused_computation.147 | convolution fusion | flops 4320132096 | bytes 18880512 | tf_op jit(solution)/shard_map/dot_general | solution.py:16
  450.5 8.3 convolution_convert_fusion.2
  459.5 64.9 %reduce-scatter.9.cloned.1.call-done = bf16[512,1024]{1,0:T(8,128)(2,1)} async-done(((bf16[2048,1024]{1,0:T(8,128)(2,1)}), bf16[512,1024]{1,0:T(8,128)(2,1)}) %reduce-scatter.9.cloned.1.call-update) | async-done | bytes 1048592 | tf_op jit(solution)/shard_map/reduce_scatter | solution.py:133
  527.4 76.5 %reduce-scatter.7.cloned.1.call-done = bf16[512,1024]{1,0:T(8,128)(2,1)} async-done(((bf16[2048,1024]{1,0:T(8,128)(2,1)}), bf16[512,1024]{1,0:T(8,128)(2,1)}) %reduce-scatter.7.cloned.1.call-update) | async-done | bytes 1048592 | tf_op jit(solution)/shard_map/reduce_scatter | solution.py:121
  611.1 23.1 %collective-permute-done = bf16[512,1024]{1,0:T(8,128)(2,1)S(1)} collective-permute-done((bf16[512,1024]{1,0:T(8,128)(2,1)S(1)}, bf16[512,1024]{1,0:T(8,128)(2,1)S(1)}, u32[]{:S(2)}, u32[]{:S(2)}) %collective-permute-start) | collective-permute-done | bytes 1048608 | tf_op jit(solution)/shard_map/ppermute | solution.py:148
  638.5 8.0 convolution_convert_fusion.5
  652.4 75.8 %collective-permute-done.1 = bf16[1024,1024]{1,0:T(8,128)(2,1)S(1)} collective-permute-done((bf16[1024,1024]{1,0:T(8,128)(2,1)S(1)}, bf16[1024,1024]{1,0:T(8,128)(2,1)S(1)}, u32[]{:S(2)}, u32[]{:S(2)}) %collective-permute-start.1) | collective-permute-done | bytes 2097184 | tf_op jit(solution)/shard_map/ppermute | solution.py:148
  738.2 191.1 %while.28 = (s32[]{:T(128)}, f32[2048,4,64]{0,2,1:T(8,128)}, f32[2048,4,64]{0,2,1:T(8,128)}, bf16[4,512,4,64]{1,3,2,0:T(8,128)(2,1)}, bf16[4,512,4,64]{1,3,2,0:T...) while((s32[]{:T(128)}, f32[2048,4,64]{0,2,1:T(8,128)}, ...), condition=%wide.region_15.16_spmd.clone, body=%wide.region_13.15_spmd.clone.sunk | while | flops 2751199232 | bytes 176625968 | solution.py:187
  744.7 7.2 fusion.167
  751.9 11.3 multiply_reduce_fusion.3
  763.3 10.9 multiply_convert_fusion.2
  774.1 7.1 fusion.168
  791.5 7.6 fusion.167
  799.2 11.3 multiply_reduce_fusion.3
  810.5 10.9 multiply_convert_fusion.2
  821.3 7.1 fusion.168
  839.5 7.6 fusion.167
  847.1 11.3 multiply_reduce_fusion.3
  858.4 10.9 multiply_convert_fusion.2
  887.4 7.6 fusion.167
  895.1 11.3 multiply_reduce_fusion.3
  906.4 10.9 multiply_convert_fusion.2
  953.1 14.6 %all-reduce.1 = (bf16[256]{0:T(256)(128)(2,1)S(1)}, bf16[256]{0:T(256)(128)(2,1)S(1)}, bf16[1024]{0:T(1024)(128)(2,1)S(1)}) all-reduce(bf16[256]{0:T(256)(128)(2,1)S(1)} %reduce_sum.195, bf16[256]{0:T(256)(128)(2,1)S(1)} %reduce_sum.197, bf16[1024]{0:T(1024)(128)(2,1)S(1)} %copy-done.43), channel_id=1, replica_groups=mesh['dp'=8,'mp'=4] {'dp'}, use_global_device_ids=true, to_apply=%region_25.26 | all-reduce | flops 1536 | bytes 6144 | tf_op jit(solution)/shard_map/psum | solution.py:224
  969.4 79.2 %all-reduce.5.cloned.1.call-done = (bf16[1024,256]{1,0:T(8,128)(2,1)}, bf16[1024,256]{1,0:T(8,128)(2,1)}, bf16[1024,256]{1,0:T(8,128)(2,1)}, bf16[256,1024]{1,0:...) async-done(((bf16[1024,256]{1,0:T(8,128)(2,1)}, bf16[1024,256]{1,0:T(8,128)(2,1)}, bf16[1024,256]{1,0:T(8,128)(2,1)}, bf16[256,1024]{1,0:T(8,128)(2,1)}, ...) | async-done | bytes 6291472 | tf_op jit(solution)/shard_map/psum | solution.py:223
  1061.2 66.7 %reduce-scatter.11.cloned.1.call-done = bf16[512,1024]{1,0:T(8,128)(2,1)} async-done(((bf16[2048,1024]{1,0:T(8,128)(2,1)}), bf16[512,1024]{1,0:T(8,128)(2,1)}) %reduce-scatter.11.cloned.1.call-update) | async-done | bytes 1048592 | tf_op jit(solution)/shard_map/reduce_scatter | solution.py:202
  1130.2 41.4 %all-reduce = (f32[1024]{0:T(1024)}, f32[1024]{0:T(1024)}, f32[1024]{0:T(1024)}, f32[1024]{0:T(1024)}, f32[1024]{0:T(1024)}, /*index=5*/f32[1024]{0:T(1024)}) all-reduce(f32[1024]{0:T(1024)S(1)} %get-tuple-element.200, f32[1024]{0:T(1024)S(1)} %get-tuple-element.205, ...), channel_id=1, replica_groups=mesh['dp'=8,'mp'=4] {'dp','mp'}, use_global_device_ids=true, to_apply=%region_20.21 | all-reduce | flops 6144 | bytes 49152 | tf_op jit(solution)/shard_map/psum | solution.py:233
  (274 shorter events, 243.9 us)
Async XLA Ops:
  7.2 341.0 %copy-start = (bf16[1024,1024]{1,0:T(8,128)(2,1)S(1)}, bf16[1024,1024]{1,0:T(8,128)(2,1)}, u32[]{:S(2)}) copy-start(bf16[1024,1024]{1,0:T(8,128)(2,1)} %param.35) | copy-start | bytes 6291460
  7.2 7.4 copy-start.51
  7.2 7.4 copy-start.52
  7.2 7.4 copy-start.17
  7.2 91.0 %all-gather.4.cloned.1.call-start = ((), (), s32[]{:S(2)}) async-start(), calls=%async_computation.4 | async-start | bytes 5242880 | tf_op jit(solution)/shard_map/all_gather | solution.py:81
  14.6 247.0 %reduce-scatter.5.cloned.1.call-start = ((), (), s32[]{:S(2)}) async-start(), calls=%async_computation.5 | async-start | bytes 5242880 | tf_op jit(solution)/shard_map/reduce_scatter | solution.py:112
  186.1 75.5 %copy-start.3 = (bf16[512,1024]{1,0:T(8,128)(2,1)S(1)}, bf16[512,1024]{1,0:T(8,128)(2,1)}, u32[]{:S(2)}) copy-start(bf16[512,1024]{1,0:T(8,128)(2,1)} %param.22) | copy-start | bytes 3145732
  186.2 162.0 %all-gather.6.cloned.1.call-start = ((), (), s32[]{:S(2)}) async-start(), calls=%async_computation.6 | async-start | bytes 5242880 | tf_op jit(solution)/shard_map/all_gather | solution.py:118
  266.8 162.1 %all-gather.8.cloned.1.call-start = ((), (), s32[]{:S(2)}) async-start(), calls=%async_computation.8 | async-start | bytes 5242880 | tf_op jit(solution)/shard_map/all_gather | solution.py:127
  267.4 257.1 %reduce-scatter.9.cloned.1.call-start = ((), (), s32[]{:S(2)}) async-start(), calls=%async_computation.9 | async-start | bytes 5242880 | tf_op jit(solution)/shard_map/reduce_scatter | solution.py:133
  449.0 154.9 %reduce-scatter.7.cloned.1.call-start = ((), (), s32[]{:S(2)}) async-start(), calls=%async_computation.7 | async-start | bytes 5242880 | tf_op jit(solution)/shard_map/reduce_scatter | solution.py:121
  458.8 65.6 %copy-start.7 = (bf16[512,1024]{1,0:T(8,128)(2,1)S(1)}, bf16[512,1024]{1,0:T(8,128)(2,1)}, u32[]{:S(2)}) copy-start(bf16[512,1024]{1,0:T(8,128)(2,1)} %reduce-scatter.5.cloned.1.call-done) | copy-start | bytes 3145732
  458.9 145.0 %copy-start.12 = (bf16[512,1024]{1,0:T(8,128)(2,1)S(1)}, bf16[512,1024]{1,0:T(8,128)(2,1)}, u32[]{:S(2)}) copy-start(bf16[512,1024]{1,0:T(8,128)(2,1)} %param.39) | copy-start | bytes 3145732
  458.9 589.8 %all-reduce.5.cloned.1.call-start = ((), (), s32[]{:S(2)}) async-start(), calls=%async_computation.11 | async-start | bytes 12582912 | tf_op jit(solution)/shard_map/psum | solution.py:223
  609.6 24.6 %collective-permute-start = (bf16[512,1024]{1,0:T(8,128)(2,1)S(1)}, bf16[512,1024]{1,0:T(8,128)(2,1)S(1)}, u32[]{:S(2)}, u32[]{:S(2)}) collective-permute-start(bf16[512,1024]{1,0:T(8,128)(2,1)S(1)} %convert_element_type.197), channel_id=1, source_target_pairs={{0,1},{1,0},{2,3},{3,2},{4,5},{5,4},{6,7},{7,6},{8,9},{9,8},{10,11... | collective-permute-start | bytes 3145736 | tf_op jit(solution)/shard_map/ppermute | solution.py:148
  611.1 27.4 %copy-start.47 = (bf16[2048,1024]{1,0:T(8,128)(2,1)S(1)}, bf16[2048,1024]{1,0:T(8,128)(2,1)}, u32[]{:S(2)}) copy-start(bf16[2048,1024]{1,0:T(8,128)(2,1)} %all-gather.8.cloned.1.call-done) | copy-start | bytes 12582916
  635.2 93.0 %copy-start.15 = (bf16[1024,1024]{1,0:T(8,128)(2,1)}, bf16[1024,1024]{1,0:T(8,128)(2,1)S(1)}, u32[]{:S(2)}) copy-start(bf16[1024,1024]{1,0:T(8,128)(2,1)S(1)} %maximum_select_fusion.1) | copy-start | bytes 6291460
  635.2 11.3 copy-start.46
  635.2 11.3 copy-start.54
  635.2 92.9 %collective-permute-start.1 = (bf16[1024,1024]{1,0:T(8,128)(2,1)S(1)}, bf16[1024,1024]{1,0:T(8,128)(2,1)S(1)}, u32[]{:S(2)}, u32[]{:S(2)}) collective-permute-start(bf16[1024,1024]{1,0:T(8,128)(2,1)S(1)} %maximum_select_fusion.1), channel_id=1, source_target_pairs={{0,2},{1,3},{2,0},{3,1},{4,6},{5,7},{6,4},{7,5},{8,10},{9,11},{10,... | collective-permute-start | bytes 6291464 | tf_op jit(solution)/shard_map/ppermute | solution.py:148
  646.5 82.9 %copy-start.21 = (bf16[256,1024]{1,0:T(8,128)(2,1)S(1)}, bf16[256,1024]{1,0:T(8,128)(2,1)}, u32[]{:S(2)}) copy-start(bf16[256,1024]{1,0:T(8,128)(2,1)} %param.31) | copy-start | bytes 1572868
  944.0 183.9 %reduce-scatter.11.cloned.1.call-start = ((), (), s32[]{:S(2)}) async-start(), calls=%async_computation.10 | async-start | bytes 5242880 | tf_op jit(solution)/shard_map/reduce_scatter | solution.py:202
  1048.7 7.5 copy-start.14
  1058.6 69.3 %copy-start.4 = (bf16[512,1024]{1,0:T(8,128)(2,1)S(1)}, bf16[512,1024]{1,0:T(8,128)(2,1)}, u32[]{:S(2)}) copy-start(bf16[512,1024]{1,0:T(8,128)(2,1)} %param.22) | copy-start | bytes 3145732
  1058.6 69.3 %copy-start.29 = (f32[1024]{0:T(1024)S(1)}, f32[1024]{0:T(1024)}, u32[]{:S(2)}) copy-start(f32[1024]{0:T(1024)} %copy-done.28) | copy-start | bytes 12292
  1058.6 69.3 %copy-start.31 = (f32[512]{0:T(512)S(1)}, f32[512]{0:T(512)}, u32[]{:S(2)}) copy-start(f32[512]{0:T(512)} %copy-done.30) | copy-start | bytes 6148
  1058.6 69.3 %copy-start.33 = (f32[512]{0:T(512)S(1)}, f32[512]{0:T(512)}, u32[]{:S(2)}) copy-start(f32[512]{0:T(512)} %copy-done.32) | copy-start | bytes 6148
  1058.7 71.5 %copy-start.34 = (f32[1024]{0:T(1024)S(1)}, f32[1024]{0:T(1024)}, u32[]{:S(2)}) copy-start(f32[1024]{0:T(1024)} %get-tuple-element.198) | copy-start | bytes 12292
  1058.7 71.5 %copy-start.35 = (f32[1024]{0:T(1024)S(1)}, f32[1024]{0:T(1024)}, u32[]{:S(2)}) copy-start(f32[1024]{0:T(1024)} %get-tuple-element.204) | copy-start | bytes 12292
  1058.7 71.5 %copy-start.36 = (f32[1024]{0:T(1024)S(1)}, f32[1024]{0:T(1024)}, u32[]{:S(2)}) copy-start(f32[1024]{0:T(1024)} %get-tuple-element.261) | copy-start | bytes 12292
  1058.7 71.5 %copy-start.37 = (f32[1024]{0:T(1024)S(1)}, f32[1024]{0:T(1024)}, u32[]{:S(2)}) copy-start(f32[1024]{0:T(1024)} %get-tuple-element.268) | copy-start | bytes 12292
  1058.7 116.8 %copy-start.1 = (bf16[1024,1024]{1,0:T(8,128)(2,1)S(1)}, bf16[1024,1024]{1,0:T(8,128)(2,1)}, u32[]{:S(2)}) copy-start(bf16[1024,1024]{1,0:T(8,128)(2,1)} %param.35) | copy-start | bytes 6291460
  (48 other events, 147.9 us)
Sparse Core Ops, SparseCore 0:
  14.7 83.4 all-gather.3
  186.3 75.2 reduce-scatter.4
  266.9 81.2 all-gather.5
  349.6 79.2 all-gather.7
  449.1 75.2 reduce-scatter.8
  526.6 77.2 reduce-scatter.6
  944.1 104.4 all-reduce.4
  1050.9 76.9 reduce-scatter.10
